TPU v7x, 256 devices: a whole 4x4x8 slice. The times are simulated.
256 devices in a mesh: blk: 8 (over x_hi, y), rep: 32 (over z, x_lo, core).
Axes of the slice: x: 4 (x_hi: 2, x_lo: 2; x = x_hi * 2 + x_lo), y: 4, z: 8, core: 2. Of those that a mesh axis runs over, the one named last changes fastest.
Arguments:
- query_hidden: bfloat16 [32, 32, 32, 768], P('rep', 'blk'), may hold values from -18 to 18
- passage_hidden: bfloat16 [32, 32, 512, 768], P('rep', 'blk'), may hold values from -6 to 6
- lengths: int32 [32, 32], P('rep', 'blk'), may hold values from 64 to 512
- projection: bfloat16 [768, 128], replicated, may hold values from -0.21875 to 0.21875
Outputs:
- query_grad: float32 [32, 32, 32, 128], P('rep', 'blk')
- passage_grad: float32 [32, 32, 512, 128], P('rep', 'blk')
- grad_weight: float32 [768, 128], replicated
- loss: float32 [], replicated
All inputs are finite; a program needn't handle non-finite values.
Results may differ from a plain program's by a relative error of at most 0.0097.
Values may be sent and summed in bfloat16 or wider, within the bound.
No kernel may reach another device: no remote copies, remote signals or barrier semaphores. Data moves between devices by JAX's collectives and lax.ppermute only.
A program may use at most 128 MiB of HBM per device.

v0:
```python
import jax
import jax.numpy as jnp
from jax import lax
from jax.sharding import PartitionSpec as P

temper = 0.5


def soft_scores(scores, lens):
    slots = scores.shape[-1]
    valid = lax.broadcasted_iota(jnp.int32, (lens.shape[0], slots), 1) < lens[:, None]
    scaled = jnp.where(valid[None], scores / temper, -jnp.inf)
    top = jnp.max(scaled, -1, keepdims=True)
    logz = top + jnp.log(jnp.sum(jnp.exp(scaled - top), -1, keepdims=True))
    pooled = temper * (logz[..., 0] - jnp.log(lens.astype(jnp.float32))[None])
    return (pooled, scaled, logz)


def cross_entropy(score, first, total):
    top = jnp.max(score, 1, keepdims=True)
    lse = top + jnp.log(jnp.sum(jnp.exp(score - top), 1, keepdims=True))
    target = lax.broadcasted_iota(jnp.int32, score.shape, 1) == first + lax.broadcasted_iota(
        jnp.int32, score.shape, 0
    )
    loss_part = jnp.sum(lse[:, 0] - jnp.sum(jnp.where(target, score, 0.0), 1))
    dscore = (jnp.exp(score - lse) - target.astype(jnp.float32)) / total
    return (loss_part, dscore)


def weighted(dscore, scaled, logz, qlen):
    spread = jnp.repeat(dscore, qlen, axis=0)
    grad_a = (spread[:, :, None] * jnp.exp(scaled - logz)).astype(jnp.bfloat16)
    return grad_a.reshape(grad_a.shape[0], -1)


def shards(query_hidden, passage_hidden, lengths, projection):
    hidden = projection.shape[0]
    nquery = query_hidden.shape[1]
    qlen = query_hidden.shape[2]
    npass = passage_hidden.shape[1]
    plen = passage_hidden.shape[2]
    groups = lax.axis_size("blk")
    total = groups * lax.axis_size("rep") * nquery
    first = lax.axis_index("blk") * nquery
    qflat = query_hidden[0].reshape(-1, hidden)
    pflat = passage_hidden[0].reshape(-1, hidden)
    qtok = jnp.dot(qflat, projection, preferred_element_type=jnp.float32).astype(jnp.bfloat16)
    ptok = jnp.dot(pflat, projection, preferred_element_type=jnp.float32).astype(jnp.bfloat16)
    every_tok = lax.all_gather(ptok, "blk", axis=0, tiled=True)
    every_len = lax.all_gather(lengths[0], "blk", axis=0, tiled=True)
    scores = jnp.dot(qtok, every_tok.T, preferred_element_type=jnp.float32).reshape(
        nquery * qlen, groups * npass, plen
    )
    pooled, scaled, logz = soft_scores(scores, every_len)
    score = jnp.sum(pooled.reshape(nquery, qlen, groups * npass), 1)
    loss_part, dscore = cross_entropy(score, first, total)
    grad_a = weighted(dscore, scaled, logz, qlen)
    qgrad = jnp.dot(grad_a, every_tok, preferred_element_type=jnp.float32)
    pgrad = lax.psum_scatter(
        jnp.dot(grad_a.T, qtok, preferred_element_type=jnp.float32),
        "blk",
        scatter_dimension=0,
        tiled=True,
    )
    wgrad = jnp.dot(qflat.T, qgrad.astype(jnp.bfloat16), preferred_element_type=jnp.float32)
    wgrad = wgrad + jnp.dot(pflat.T, pgrad.astype(jnp.bfloat16), preferred_element_type=jnp.float32)
    wgrad, loss_sum = lax.psum((wgrad, loss_part), ("blk", "rep"))
    query_grad = qgrad.reshape(1, nquery, qlen, -1)
    passage_grad = pgrad.reshape(1, npass, plen, -1)
    return (query_grad, passage_grad, wgrad, loss_sum / total)


def solution(mesh):
    return jax.shard_map(
        shards,
        mesh=mesh,
        in_specs=(P("rep", "blk", None, None), P("rep", "blk", None, None), P("rep", "blk"), P()),
        out_specs=(P("rep", "blk", None, None), P("rep", "blk", None, None), P(), P()),
        check_vma=False,
    )
```

profile of v0, /device:TPU:1, one launch (start us, length us, event | category | flops | bytes accessed | tf_op | source)
XLA Modules:
  0.0 521.1 jit_solution(17235841440828739490)
XLA Ops:
  7.2 1.8 copy-done
  9.1 2.7 convolution_convert_fusion
  11.9 1.3 dynamic-slice
  13.8 0.8 bitcast_dynamic-update-slice_fusion
  14.6 11.6 %all-reduce = s32[32]{0:T(128)S(1)} all-reduce(s32[32]{0:T(128)S(1)} %bitcast_dynamic-update-slice_fusion), channel_id=2, replica_groups=mesh['blk'=8,'rep'=32] {'blk'}, use_global_device_ids=true, to_apply=%add | all-reduce | flops 32 | bytes 256 | tf_op jit(solution)/shard_map/all_gather | solution.py:50
  26.4 1.2 convolution_convert_fusion.1
  27.6 64.1 %all-gather.3.cloned.1.call-done = bf16[16384,128]{1,0:T(8,128)(2,1)} async-done(((bf16[2048,128]{1,0:T(8,128)(2,1)}), bf16[16384,128]{1,0:T(8,128)(2,1)}) %all-gather.3.cloned.1.call-update) | async-done | bytes 4194320 | tf_op jit(solution)/shard_map/all_gather | solution.py:49
  91.8 3.4 convolution_multiply_fusion
  95.2 6.5 %copy.9 = f32[16,8,32,512]{3,2,1,0:T(8,128)S(1)} copy(f32[16,8,32,512]{3,1,2,0:T(8,128)S(1)} %bitcast.36) | data formatting | bytes 16777216
  102.5 2.3 exponential_reduce_fusion
  105.8 0.7 mul.27
  106.5 9.7 %copy.10 = f32[16,8,32,512]{3,1,2,0:T(8,128)} copy(f32[16,8,32,512]{3,2,1,0:T(8,128)S(1)} %bitcast.43) | data formatting | bytes 16777216
  116.2 0.9 sub.59
  117.2 9.8 %copy.12 = f32[16,8,32,512]{3,1,2,0:T(8,128)} copy(f32[16,8,32,512]{3,2,1,0:T(8,128)S(1)} %bitcast.44) | data formatting | bytes 16777216
  126.9 7.0 %multiply_convert_fusion = bf16[128,16384]{1,0:T(8,128)(2,1)S(1)} fusion(f32[128,16384]{1,0:T(8,128)} %bitcast.41, f32[128,16384]{1,0:T(8,128)} %bitcast.42, f32[128,16384]{1,0:T(8,128)S(1)} %bitcast.38, pred[16384]{0:T(1024)(128)(4,1)S(1)} %lt.23), kind=kLoop, calls=%fused_computation.1 | loop fusion | flops 8388608 | bytes 29376512 | tf_op jit(solution)/shard_map/convert_element_type | solution.py:32
  134.0 2.0 copy-done.2
  136.0 4.5 fusion.5
  140.6 4.7 fusion.4
  145.3 112.7 %reduce-scatter.2.cloned.1.call-done = f32[2048,128]{1,0:T(8,128)} async-done(((f32[16384,128]{1,0:T(8,128)}), f32[2048,128]{1,0:T(8,128)}) %reduce-scatter.2.cloned.1.call-update) | async-done | bytes 1048592 | tf_op jit(solution)/shard_map/reduce_scatter | solution.py:59
  258.1 1.8 fusion.1
  259.9 1.0 fusion
  260.9 74.6 %psum.15 = f32[]{:T(128)} all-reduce(f32[]{:T(128)} %get-tuple-element.10), channel_id=1, replica_groups=mesh['blk'=8,'rep'=32] {'blk','rep'}, use_global_device_ids=true, to_apply=%region_9.10 | all-reduce | flops 1 | bytes 8 | tf_op jit(solution)/shard_map/psum | solution.py:67
  336.2 175.4 %all-reduce.3.cloned.1.call-done = f32[768,128]{0,1:T(8,128)} async-done(((f32[768,128]{0,1:T(8,128)}), f32[768,128]{0,1:T(8,128)}) %all-reduce.3.cloned.1.call-update) | async-done | bytes 393232 | tf_op jit(solution)/shard_map/psum | solution.py:67
  511.5 1.9 copy.8
  (34 shorter events, 2.2 us)
Async XLA Ops:
  7.2 1.9 copy-start
  7.2 84.6 %all-gather.3.cloned.1.call-start = ((), (), s32[]{:S(2)}) async-start(), calls=%async_computation.1 | async-start | bytes 4718592 | tf_op jit(solution)/shard_map/all_gather | solution.py:49
  11.8 246.3 %reduce-scatter.2.cloned.1.call-start = ((), (), s32[]{:S(2)}) async-start(), calls=%async_computation.2 | async-start | bytes 9437184 | tf_op jit(solution)/shard_map/reduce_scatter | solution.py:59
  95.2 6.5 %copy-start.1 = (f32[128,16384]{1,0:T(8,128)}, f32[128,16384]{1,0:T(8,128)S(1)}, u32[]{:S(2)}) copy-start(f32[128,16384]{1,0:T(8,128)S(1)} %convolution_multiply_fusion) | copy-start | bytes 25165828
  116.2 10.7 %slice-start = ((s8[8388608]{0:T(1024)(128)(4,1)}), s8[4194304]{0:T(1024)(128)(4,1)S(1)}, s32[]{:S(2)}) async-start(s8[8388608]{0:T(1024)(128)(4,1)} %bitcast.37), calls=%async_computation.4 | async-start | bytes 8388608
  117.2 9.8 %slice-start.1 = ((s8[8388608]{0:T(1024)(128)(4,1)}), s8[4194304]{0:T(1024)(128)(4,1)S(1)}, s32[]{:S(2)}) async-start(s8[8388608]{0:T(1024)(128)(4,1)} %bitcast.37), calls=%async_computation.5 | async-start | bytes 8388608
  134.0 2.0 copy-start.2
  140.5 119.4 %copy-start.3 = (bf16[1,4,32,768]{3,2,1,0:T(8,128)(2,1)S(1)}, bf16[1,4,32,768]{3,2,1,0:T(8,128)(2,1)}, u32[]{:S(2)}) copy-start(bf16[1,4,32,768]{3,2,1,0:T(8,128)(2,1)} %param.4) | copy-start | bytes 589828
  140.5 371.0 %all-reduce.3.cloned.1.call-start = ((), (), s32[]{:S(2)}) async-start(), calls=%async_computation.3 | async-start | bytes 786432 | tf_op jit(solution)/shard_map/psum | solution.py:67
  145.3 368.1 %copy-start.4 = (f32[128,128]{1,0:T(8,128)}, f32[128,128]{1,0:T(8,128)S(1)}, u32[]{:S(2)}) copy-start(f32[128,128]{1,0:T(8,128)S(1)} %fusion.4) | copy-start | bytes 196612
Sparse Core Ops, SparseCore 0:
  11.9 79.8 all-gather.2
  140.6 117.3 reduce-scatter.1
  265.1 246.4 all-reduce.2
where the time goes:
time: 522 us; the launch traced here: 521 us
  waiting for transfers between devices  352 us (67%)
  blocking collectives  86.2 us (17%)
  local copies, waits for them, and re-layouts  35.5 us (7%)
  matrix products  19.4 us (4%)
  between operations  16.4 us (3%)
  other arithmetic  11.2 us (2%)
    psum x1, waiting for transfers between devices, shards(): wgrad, loss_sum = lax.psum((wgrad, loss_part), ('blk', 'rep'))  175 us
    reduce_scatter x1, waiting for transfers between devices, shards(): lax.psum_scatter(jnp.dot(grad_a.T, qtok, preferred_element_type=jnp.float...  113 us
    psum x1, blocking collectives, shards(): wgrad, loss_sum = lax.psum((wgrad, loss_part), ('blk', 'rep'))  74.6 us
    all_gather x1, waiting for transfers between devices, shards(): every_tok = lax.all_gather(ptok, 'blk', axis=0, tiled=True)  64.1 us
    unnamed x23, local copies, waits for them, and re-layouts  33.8 us
    all_gather x1, blocking collectives, shards(): every_len = lax.all_gather(lengths[0], 'blk', axis=0, tiled=True)  11.6 us
  transfers between devices with their start and end apart: 3, of which 3 were waited for; matrix products, arithmetic and copies ran while one was open for 2% of the time, Pallas kernels for 0%

commit v1 on v0

--- a/solution.py
+++ b/solution.py
@@ -46,7 +46,9 @@
     pflat = passage_hidden[0].reshape(-1, hidden)
     qtok = jnp.dot(qflat, projection, preferred_element_type=jnp.float32).astype(jnp.bfloat16)
     ptok = jnp.dot(pflat, projection, preferred_element_type=jnp.float32).astype(jnp.bfloat16)
-    every_tok = lax.all_gather(ptok, "blk", axis=0, tiled=True)
+    every_tok = jnp.concatenate(
+        lax.all_to_all(jnp.stack([ptok] * lax.axis_size("blk")), "blk", 0, 0), axis=0
+    )
     every_len = lax.all_gather(lengths[0], "blk", axis=0, tiled=True)
     scores = jnp.dot(qtok, every_tok.T, preferred_element_type=jnp.float32).reshape(
         nquery * qlen, groups * npass, plen

time: 522 us -> 489 us (0.937)
  waiting for transfers between devices: 352 us -> 290 us
  blocking collectives: 86.2 us -> 128 us
  local copies, waits for them, and re-layouts: 35.5 us -> 14.2 us
  starting transfers between devices: 0.12 us -> 7.7 us
    all_gather x1 -> x0, waiting for transfers between devices: 64.1 us -> none  [shards(): every_tok = lax.all_gather(ptok, 'blk', axis=0, tiled=True)]
    all_gather x1, blocking collectives: 11.6 us -> 53.2 us  [shards(): every_len = lax.all_gather(lengths[0], 'blk', axis=0, tiled=True)]
    unnamed x23 -> x26, local copies, waits for them, and re-layouts: 33.8 us -> 5.03 us
    all_to_all x0 -> x1, starting transfers between devices: none -> 7.62 us  [shards(): lax.all_to_all(jnp.stack([ptok] * lax.axis_size('blk')), 'blk', 0, 0)]
    convert_element_type x0 -> x1, local copies, waits for them, and re-layouts: none -> 6.39 us  [weighted(): grad_a = (spread[:, :, None] * jnp.exp(scaled - logz)).astype(jnp.bfloat16)]
  transfers between devices with their start and end apart: 3 -> 3, of which waited for: 3 -> 2; matrix products, arithmetic and copies ran while one was open for 2% -> 2% of each run, Pallas kernels for 0% -> 0%
where the time goes in v1:
time: 489 us; the launch traced here: 488 us
  waiting for transfers between devices  290 us (59%)
  blocking collectives  128 us (26%)
  matrix products  20.5 us (4%)
  between operations  16.6 us (3%)
  local copies, waits for them, and re-layouts  14.2 us (3%)
  other arithmetic  11.2 us (2%)
  starting transfers between devices  7.7 us (2%)
    psum x1, waiting for transfers between devices, shards(): wgrad, loss_sum = lax.psum((wgrad, loss_part), ('blk', 'rep'))  175 us
    reduce_scatter x1, waiting for transfers between devices, shards(): lax.psum_scatter(jnp.dot(grad_a.T, qtok, preferred_element_type=jnp.float...  115 us
    psum x1, blocking collectives, shards(): wgrad, loss_sum = lax.psum((wgrad, loss_part), ('blk', 'rep'))  74.6 us
    all_gather x1, blocking collectives, shards(): every_len = lax.all_gather(lengths[0], 'blk', axis=0, tiled=True)  53.2 us
  transfers between devices with their start and end apart: 3, of which 2 were waited for; matrix products, arithmetic and copies ran while one was open for 2% of the time, Pallas kernels for 0%

profile of v1, /device:TPU:1, one launch (start us, length us, event | category | flops | bytes accessed | tf_op | source)
XLA Modules:
  0.0 488.0 jit_solution(17336181360967730487)
XLA Ops:
  7.2 1.9 copy-done
  9.1 1.9 convolution_convert_fusion
  11.0 2.5 stack.2
  13.4 7.6 %all-to-all-start = ((bf16[8,2048,128]{2,1,0:T(8,128)(2,1)}), bf16[8,2048,128]{2,1,0:T(8,128)(2,1)}, u32[]{:S(2)}, u32[]{:S(2)}) async-start(bf16[8,2048,128]{2,1,0:T(8,128)(2,1)} %stack.2), calls=%async_computation | async-start | bytes 8388608 | tf_op jit(solution)/shard_map/all_to_all | solution.py:50
  21.1 0.6 dynamic-slice
  22.5 53.2 %all-reduce = s32[32]{0:T(128)S(1)} all-reduce(s32[32]{0:T(128)S(1)} %bitcast_dynamic-update-slice_fusion), channel_id=2, replica_groups=mesh['blk'=8,'rep'=32] {'blk'}, use_global_device_ids=true, to_apply=%add | all-reduce | flops 32 | bytes 256 | tf_op jit(solution)/shard_map/all_gather | solution.py:52
  75.7 0.5 iota_add_fusion
  76.2 0.5 convert_log_fusion
  76.7 0.7 iota_compare_fusion
  77.5 0.8 convolution_convert_fusion.1
  78.3 3.5 fusion
  81.9 2.7 exponential_reduce_fusion
  84.6 0.5 copy-done.1
  85.5 0.6 subtract_reduce_fusion
  86.3 5.9 %multiply_convert_fusion = bf16[128,32,512]{2,0,1:T(8,128)(2,1)} fusion(f32[128,32,512]{2,0,1:T(8,128)} %copy-done.1, f32[128,32]{0,1:T(8,128)S(1)} %log_add_fusion, f32[128,32]{0,1:T(8,128)S(1)} %mul.23, pred[32,512]{1,0:T(8,128)(4,1)S(1)} %iota_compare_fusion), kind=kLoop, calls=%fused_computation | loop fusion | flops 10485760 | bytes 12632064 | tf_op jit(solution)/shard_map/convert_element_type | solution.py:32
  92.2 6.4 %copy.9 = bf16[128,32,512]{0,2,1:T(8,128)(2,1)} copy(bf16[128,32,512]{2,0,1:T(8,128)(2,1)} %multiply_convert_fusion) | data formatting | bytes 8388608 | tf_op jit(solution)/shard_map/convert_element_type | solution.py:32
  98.6 6.6 %fusion.8 = f32[16384,128]{1,0:T(8,128)} fusion(bf16[128,16384]{0,1:T(8,128)(2,1)} %bitcast.34, bf16[128,128]{1,0:T(8,128)(2,1)S(1)} %copy-done.4), kind=kOutput, calls=%fused_computation.26 | convolution fusion | flops 536870912 | bytes 12615680 | tf_op jit(solution)/shard_map/dot_general | solution.py:62
  105.3 4.8 fusion.7
  110.1 114.6 %reduce-scatter.2.cloned.1.call-done = f32[2048,128]{1,0:T(8,128)} async-done(((f32[16384,128]{1,0:T(8,128)}), f32[2048,128]{1,0:T(8,128)}) %reduce-scatter.2.cloned.1.call-update) | async-done | bytes 1048592 | tf_op jit(solution)/shard_map/reduce_scatter | solution.py:61
  224.6 1.8 fusion.2
  226.5 1.0 fusion.1
  227.5 74.6 %psum.15 = f32[]{:T(128)} all-reduce(f32[]{:T(128)} %get-tuple-element.14), channel_id=1, replica_groups=mesh['blk'=8,'rep'=32] {'blk','rep'}, use_global_device_ids=true, to_apply=%region_9.10 | all-reduce | flops 1 | bytes 8 | tf_op jit(solution)/shard_map/psum | solution.py:69
  302.7 175.3 %all-reduce.3.cloned.1.call-done = f32[768,128]{0,1:T(8,128)} async-done(((f32[768,128]{0,1:T(8,128)}), f32[768,128]{0,1:T(8,128)}) %all-reduce.3.cloned.1.call-update) | async-done | bytes 393232 | tf_op jit(solution)/shard_map/psum | solution.py:69
  478.1 1.9 copy.10
  (35 shorter events, 0.8 us)
Async XLA Ops:
  7.2 1.9 copy-start
  13.4 7.7 %copy-start.10 = (u32[256]{0:T(256)S(1)}, u32[256]{0:T(256)}, u32[]{:S(2)}) copy-start(u32[256]{0:T(256)} %constant.27) | copy-start | bytes 3076
  13.4 8.9 %copy-start.9 = (s32[1,4]{1,0:T(1,128)S(1)}, s32[1,4]{1,0:T(1,128)}, u32[]{:S(2)}) copy-start(s32[1,4]{1,0:T(1,128)} %param.6) | copy-start | bytes 52
  13.4 64.0 %copy-start.2 = (bf16[768,128]{1,0:T(8,128)(2,1)S(1)}, bf16[768,128]{1,0:T(8,128)(2,1)}, u32[]{:S(2)}) copy-start(bf16[768,128]{1,0:T(8,128)(2,1)} %param.7) | copy-start | bytes 589828
  13.4 64.1 %copy-start.3 = (bf16[1,4,32,768]{3,2,1,0:T(8,128)(2,1)S(1)}, bf16[1,4,32,768]{3,2,1,0:T(8,128)(2,1)}, u32[]{:S(2)}) copy-start(bf16[1,4,32,768]{3,2,1,0:T(8,128)(2,1)} %param.4) | copy-start | bytes 589828
  13.4 64.9 %all-to-all-start = ((bf16[8,2048,128]{2,1,0:T(8,128)(2,1)}), bf16[8,2048,128]{2,1,0:T(8,128)(2,1)}, u32[]{:S(2)}, u32[]{:S(2)}) async-start(bf16[8,2048,128]{2,1,0:T(8,128)(2,1)} %stack.2), calls=%async_computation | async-start | bytes 8388608 | tf_op jit(solution)/shard_map/all_to_all | solution.py:50
  21.1 203.6 %reduce-scatter.2.cloned.1.call-start = ((), (), s32[]{:S(2)}) async-start(), calls=%async_computation.2 | async-start | bytes 9437184 | tf_op jit(solution)/shard_map/reduce_scatter | solution.py:61
  75.7 0.5 copy-start.8
  81.9 3.2 copy-start.1
  81.9 3.3 copy-start.7
  81.9 3.5 copy-start.6
  92.2 6.4 %copy-start.4 = (bf16[128,128]{1,0:T(8,128)(2,1)S(1)}, bf16[128,128]{1,0:T(8,128)(2,1)}, u32[]{:S(2)}) copy-start(bf16[128,128]{1,0:T(8,128)(2,1)} %convolution_convert_fusion.1) | copy-start | bytes 98308
  105.2 372.8 %all-reduce.3.cloned.1.call-start = ((), (), s32[]{:S(2)}) async-start(), calls=%async_computation.3 | async-start | bytes 786432 | tf_op jit(solution)/shard_map/psum | solution.py:69
  110.0 369.9 %copy-start.5 = (f32[128,128]{1,0:T(8,128)}, f32[128,128]{1,0:T(8,128)S(1)}, u32[]{:S(2)}) copy-start(f32[128,128]{1,0:T(8,128)S(1)} %fusion.7) | copy-start | bytes 196612
Sparse Core Ops, SparseCore 0:
  105.4 119.2 reduce-scatter.1
  231.6 246.3 all-reduce.2
